TPU v7x, 256 devices: a whole 4x4x8 slice. The times are simulated.
256 devices in a mesh: rows: 64 (over z, y, core), rep: 4 (over x).
Axes of the slice: x: 4, y: 4, z: 8, core: 2. Of those that a mesh axis runs over, the one named last changes fastest.
Arguments:
- features: bfloat16 [262144, 256], P(('rows', 'rep')), may hold values from -6 to 6
- weight: bfloat16 [256, 256], replicated, may hold values from -0.375 to 0.375
- block_cols: int32 [2048, 4, 2], P('rows', 'rep'), may hold values from 0 to 511, as said below
- block_vals: bfloat16 [2048, 4, 2, 128, 128], P('rows', 'rep'), as said below
- out_grad: bfloat16 [262144, 256], P('rows'), may hold values from -6 to 6
Outputs:
- activations: bfloat16 [262144, 256], P(('rows', 'rep'))
- input_grad: bfloat16 [262144, 256], P(('rows', 'rep'))
- weight_grad: float32 [256, 256], replicated
Inputs may be any that keep to these rules, and one draw needn't show every extreme that they name: `block_cols`: layer c's k-th block column is global block column (k // 8) * 32 + c * 8 + k % 8, whose rows the device of index k // 8 along rows holds in layer c. In the layer that owns a block row, slot 0 is its diagonal block; no other held block of a device lies in its own block columns. For every layer, every device along rows and every other device along rows, at most 1 of the first device's held blocks in that layer lie in block columns of the other, and in every draw some pair has exactly 1. `block_vals`: the adjacency is symmetric: every held block at block row b, block column g in slot s has a partner held at block row g, block column b in slot s (of the layer owning b) that is its transpose; diagonal blocks are symmetric.
All inputs are finite; a program needn't handle non-finite values.
Results may differ from a plain program's by a relative error of at most 0.006.
Values may be sent and summed in bfloat16 or wider, within the bound.
A program may use at most 128 MiB of HBM per device.

v0:
```python
import math
import jax
import jax.numpy as jnp
from jax import lax
from jax.sharding import PartitionSpec as P


def silu_parts(summed):
    sigmoid_vals = jax.nn.sigmoid(summed)
    return (summed * sigmoid_vals, sigmoid_vals * (1.0 + summed * (1.0 - sigmoid_vals)))


def apply_blocks(local_vals, fetched):
    product = jnp.einsum("bsij,bsjf->bif", local_vals, fetched, preferred_element_type=jnp.float32)
    return product.reshape(-1, fetched.shape[-1])


def serve_blocks(source_rows, asked_places, block_size):
    feature_width = source_rows.shape[1]
    blocks = source_rows.reshape(-1, block_size, feature_width)
    flat_ask = asked_places.reshape(-1)
    picked = jnp.take(blocks, jnp.clip(flat_ask, 0, blocks.shape[0] - 1), axis=0)
    picked = jnp.where((flat_ask >= 0)[:, None, None], picked, jnp.zeros_like(picked))
    return picked


def on_device(features, weight, block_cols, block_vals, out_grad):
    own_rows, feature_width = features.shape
    block_size = block_vals.shape[-1]
    row_blocks, slot_count = (block_cols.shape[0], block_cols.shape[2])
    own_blocks = own_rows // block_size
    peer_count = lax.axis_size("rows")
    layer_count = lax.axis_size("rep")
    couple_total = ((layer_count - 1) * slot_count * own_blocks + own_blocks) // 2
    reach_classes = peer_count // 2 - 1
    capacity = (couple_total + reach_classes - 1) // reach_classes
    my_group = lax.axis_index("rows")
    layer_index = lax.axis_index("rep")
    local_vals = block_vals[:, 0]
    flat_cols = block_cols[:, 0].reshape(-1)
    request_total = flat_cols.shape[0]
    owners = flat_cols // own_blocks
    places = flat_cols % own_blocks
    remote = owners != my_group
    positions = jnp.arange(request_total, dtype=jnp.int32)
    same_owner = (owners[:, None] == owners[None, :]) & (positions[:, None] > positions[None, :])
    owner_ranks = jnp.sum(same_owner.astype(jnp.int32), axis=1)
    slot_keys = jnp.where(remote, owners * capacity + owner_ranks, -1)
    slot_table = jnp.arange(peer_count * capacity, dtype=jnp.int32)
    matches = slot_keys[:, None] == slot_table[None, :]
    requests = (jnp.sum(jnp.where(matches, places[:, None] + 1, 0), axis=0) - 1).reshape(
        peer_count, capacity
    )
    asked_places = lax.all_to_all(requests, "rows", split_axis=0, concat_axis=0, tiled=True)
    mixed_rows = jnp.dot(features, weight, preferred_element_type=jnp.float32).astype(jnp.bfloat16)
    arrived = lax.all_to_all(
        serve_blocks(mixed_rows, asked_places, block_size),
        "rows",
        split_axis=0,
        concat_axis=0,
        tiled=True,
    )
    from_peers = jnp.take(arrived, jnp.clip(slot_keys, 0, arrived.shape[0] - 1), axis=0)
    from_self = jnp.take(mixed_rows.reshape(own_blocks, block_size, feature_width), places, axis=0)
    joined = jnp.where(remote[:, None, None], from_peers, from_self)
    partial_sum = apply_blocks(
        local_vals, joined.reshape(row_blocks, slot_count, block_size, feature_width)
    )
    share_start = layer_index * own_rows
    summed = lax.psum(partial_sum, "rep")
    values_all, slopes_all = silu_parts(summed)
    grad_rows = (out_grad.astype(jnp.float32) * slopes_all).astype(jnp.bfloat16)
    activated = lax.dynamic_slice_in_dim(values_all, share_start, own_rows, 0).astype(jnp.bfloat16)
    slot_terms = jnp.einsum(
        "bsji,bjf->bsif",
        local_vals,
        grad_rows.reshape(row_blocks, block_size, feature_width),
        preferred_element_type=jnp.float32,
    ).reshape(request_total, block_size, feature_width)
    filler = jnp.sum(jnp.where(matches, positions[:, None], 0), axis=0)
    filled = jnp.any(matches, axis=0)
    outgoing = jnp.where(
        filled[:, None, None], jnp.take(slot_terms, filler, axis=0), jnp.zeros((), jnp.float32)
    )
    returned = lax.all_to_all(outgoing, "rows", split_axis=0, concat_axis=0, tiled=True)
    block_span = block_size * feature_width
    own_index = jnp.arange(own_blocks, dtype=jnp.int32)
    arrive_hot = (asked_places.reshape(-1)[:, None] == own_index[None, :]).astype(jnp.float32)
    self_hot = ((~remote)[:, None] & (places[:, None] == own_index[None, :])).astype(jnp.float32)
    collected = jnp.einsum(
        "qo,qx->ox", arrive_hot, returned.reshape(-1, block_span), precision=lax.Precision.HIGHEST
    )
    self_terms = jnp.einsum(
        "no,nx->ox", self_hot, slot_terms.reshape(-1, block_span), precision=lax.Precision.HIGHEST
    )
    back_rows = (collected + self_terms).reshape(own_rows, feature_width)
    node_total = own_rows * peer_count * layer_count
    local_weight = jnp.dot(
        features.astype(jnp.float32).T, back_rows, precision=lax.Precision.HIGHEST
    )
    weight_grad = lax.psum(local_weight, ("rows", "rep")) * (1.0 / math.sqrt(node_total))
    input_grad = jnp.dot(
        back_rows.astype(jnp.bfloat16), weight.T, preferred_element_type=jnp.float32
    ).astype(jnp.bfloat16)
    return (activated, input_grad, weight_grad)


def solution(mesh):
    placed = (
        P(("rows", "rep"), None),
        P(),
        P("rows", "rep", None),
        P("rows", "rep", None, None, None),
        P("rows", None),
    )
    return jax.shard_map(
        on_device,
        mesh=mesh,
        in_specs=placed,
        out_specs=(P(("rows", "rep"), None), P(("rows", "rep"), None), P()),
        check_vma=False,
    )
```

profile of v0, /device:TPU:2, one launch (start us, length us, event | category | flops | bytes accessed | tf_op | source)
XLA Modules:
  0.0 755.1 jit_solution(3216159301547902736)
XLA Ops:
  7.2 0.9 copy.37
  9.3 12.1 %all-to-all-start = ((s32[64,1,1]{2,1,0:T(1,128)}), s32[64,1,1]{2,1,0:T(1,128)S(1)}, u32[]{:S(2)}, u32[]{:S(2)}) async-start(s32[64,1,1]{2,1,0:T(1,128)} %copy.38), calls=%async_computation | async-start | bytes 65536 | tf_op jit(solution)/shard_map/all_to_all | solution.py:54
  21.4 1.4 convolution_convert_fusion.1
  22.7 8.2 %all-to-all-done = s32[64,1,1]{2,1,0:T(1,128)S(1)} async-done(((s32[64,1,1]{2,1,0:T(1,128)}), s32[64,1,1]{2,1,0:T(1,128)S(1)}, u32[]{:S(2)}, u32[]{:S(2)}) %all-to-all-start) | async-done | bytes 288 | tf_op jit(solution)/shard_map/all_to_all | solution.py:54
  30.9 1.2 reduce.1
  32.1 2.8 gather_fusion.2
  34.9 1.2 compare_reduce_fusion
  36.1 4.0 select_select_fusion.2
  40.1 5.7 all-to-all-start.1
  46.1 2.8 gather_fusion.3
  48.9 93.1 %all-to-all-done.1 = bf16[64,128,256]{2,1,0:T(8,128)(2,1)} async-done(((bf16[64,128,256]{2,1,0:T(8,128)(2,1)}), bf16[64,128,256]{2,1,0:T(8,128)(2,1)}, u32[]{:S(2)}, u32[]{:S(2)}) %all-to-all-start.1) | async-done | bytes 4194336 | tf_op jit(solution)/shard_map/all_to_all | solution.py:56
  142.0 5.0 gather_fusion
  147.0 4.1 select_select_fusion.1
  151.0 2.8 fusion.2
  154.0 92.9 %all-reduce.3.cloned.1.call-done = f32[4096,256]{1,0:T(8,128)} async-done(((f32[4096,256]{1,0:T(8,128)}), f32[4096,256]{1,0:T(8,128)}) %all-reduce.3.cloned.1.call-update) | async-done | bytes 4194320 | tf_op jit(solution)/shard_map/psum | solution.py:70
  246.9 6.4 multiply_convert_fusion
  253.3 4.5 fusion
  257.9 9.0 %copy.41 = f32[64,128,256]{2,1,0:T(8,128)} copy(f32[64,128,256]{1,2,0:T(8,128)} %bitcast.59) | data formatting | bytes 16777216 | tf_op jit(solution)/shard_map/reshape | solution.py:79
  266.9 7.7 %gather_fusion.1 = f32[64,128,256]{2,1,0:T(8,128)} fusion(f32[64,128,256]{2,1,0:T(8,128)} %copy.41, s32[1024]{0:T(1024)S(1)} %pad_clamp_fusion), kind=kCustom, calls=%fused_computation.3 | custom fusion | bytes 16777472 | tf_op jit(solution)/shard_map/jit(_take)/gather | solution.py:83
  274.5 8.5 %select_select_fusion = f32[64,128,256]{2,1,0:T(8,128)} fusion(f32[64,128,256]{2,1,0:T(8,128)} %gather_fusion.1, pred[64]{0:T(512)(128)(4,1)S(1)} %compare_and_fusion.2, pred[64]{0:T(512)(128)(4,1)S(1)} %fusion.6), kind=kLoop, calls=%fused_computation.5 | loop fusion | flops 4194304 | bytes 16777344 | tf_op jit(solution)/shard_map/jit(_where)/select_n | solution.py:82
  283.0 10.7 %all-to-all-start.2 = ((f32[64,128,256]{2,1,0:T(8,128)}), f32[64,128,256]{2,1,0:T(8,128)}, u32[]{:S(2)}, u32[]{:S(2)}) async-start(f32[64,128,256]{2,1,0:T(8,128)} %select_select_fusion), calls=%async_computation.2 | async-start | bytes 16777216 | tf_op jit(solution)/shard_map/all_to_all | solution.py:85
  293.8 9.2 %copy.49 = f32[8,8,128,256]{3,1,2,0:T(8,128)} copy(f32[8,8,128,256]{2,3,1,0:T(8,128)} %bitcast.60) | data formatting | bytes 16777216
  303.0 2.4 fusion.4
  305.5 174.4 %all-to-all-done.2 = f32[64,128,256]{2,1,0:T(8,128)} async-done(((f32[64,128,256]{2,1,0:T(8,128)}), f32[64,128,256]{2,1,0:T(8,128)}, u32[]{:S(2)}, u32[]{:S(2)}) %all-to-all-start.2) | async-done | bytes 8388640 | tf_op jit(solution)/shard_map/all_to_all | solution.py:85
  479.9 8.3 %copy.48 = f32[8,8,128,256]{3,1,2,0:T(8,128)S(1)} copy(f32[8,8,128,256]{3,2,1,0:T(8,128)} %bitcast.25) | data formatting | bytes 16777216
  488.1 2.9 fusion.8
  491.1 3.9 convolution_add_fusion
  494.9 1.4 reshape.298
  496.4 2.7 convolution_bitcast_fusion
  499.1 1.1 convolution_convert_fusion
  500.3 246.2 %all-reduce.5.cloned.1.call-done = f32[256,256]{0,1:T(8,128)} async-done(((f32[256,256]{0,1:T(8,128)}), f32[256,256]{0,1:T(8,128)}) %all-reduce.5.cloned.1.call-update) | async-done | bytes 262160 | tf_op jit(solution)/shard_map/psum | solution.py:101
  746.4 1.0 broadcast_multiply_fusion
  (34 shorter events, 2.6 us)
Async XLA Ops:
  7.2 143.9 %copy-start = (bf16[32,1,2,128,128]{4,3,2,1,0:T(8,128)(2,1)S(1)}, bf16[32,1,2,128,128]{4,3,2,1,0:T(8,128)(2,1)}, u32[]{:S(2)}) copy-start(bf16[32,1,2,128,128]{4,3,2,1,0:T(8,128)(2,1)} %param.10) | copy-start | bytes 6291460
  9.3 21.6 %all-to-all-start = ((s32[64,1,1]{2,1,0:T(1,128)}), s32[64,1,1]{2,1,0:T(1,128)S(1)}, u32[]{:S(2)}, u32[]{:S(2)}) async-start(s32[64,1,1]{2,1,0:T(1,128)} %copy.38), calls=%async_computation | async-start | bytes 65536 | tf_op jit(solution)/shard_map/all_to_all | solution.py:54
  40.1 101.9 %all-to-all-start.1 = ((bf16[64,128,256]{2,1,0:T(8,128)(2,1)}), bf16[64,128,256]{2,1,0:T(8,128)(2,1)}, u32[]{:S(2)}, u32[]{:S(2)}) async-start(bf16[64,128,256]{2,1,0:T(8,128)(2,1)} %select_select_fusion.2), calls=%async_computation.1 | async-start | bytes 8388608 | tf_op jit(solution)/shard_map/all_to_all | solution.py:56
  45.8 201.1 %all-reduce.3.cloned.1.call-start = ((), (), s32[]{:S(2)}) async-start(), calls=%async_computation.3 | async-start | bytes 8388608 | tf_op jit(solution)/shard_map/psum | solution.py:70
  283.0 196.8 %all-to-all-start.2 = ((f32[64,128,256]{2,1,0:T(8,128)}), f32[64,128,256]{2,1,0:T(8,128)}, u32[]{:S(2)}, u32[]{:S(2)}) async-start(f32[64,128,256]{2,1,0:T(8,128)} %select_select_fusion), calls=%async_computation.2 | async-start | bytes 16777216 | tf_op jit(solution)/shard_map/all_to_all | solution.py:85
  293.8 452.7 %all-reduce.5.cloned.1.call-start = ((), (), s32[]{:S(2)}) async-start(), calls=%async_computation.4 | async-start | bytes 524288 | tf_op jit(solution)/shard_map/psum | solution.py:101
  479.8 11.2 %slice-start = ((s8[8388608]{0:T(1024)(128)(4,1)}), s8[4194304]{0:T(1024)(128)(4,1)S(1)}, s32[]{:S(2)}) async-start(s8[8388608]{0:T(1024)(128)(4,1)} %bitcast.63), calls=%async_computation.5 | async-start | bytes 8388608
  479.9 11.2 %slice-start.1 = ((s8[8388608]{0:T(1024)(128)(4,1)}), s8[4194304]{0:T(1024)(128)(4,1)S(1)}, s32[]{:S(2)}) async-start(s8[8388608]{0:T(1024)(128)(4,1)} %bitcast.63), calls=%async_computation.6 | async-start | bytes 8388608
  491.0 257.2 %copy-start.1 = (bf16[32,1,2,128,128]{4,3,2,1,0:T(8,128)(2,1)S(1)}, bf16[32,1,2,128,128]{4,3,2,1,0:T(8,128)(2,1)}, u32[]{:S(2)}) copy-start(bf16[32,1,2,128,128]{4,3,2,1,0:T(8,128)(2,1)} %param.10) | copy-start | bytes 6291460
  494.9 4.2 copy-start.2
Sparse Core Ops, SparseCore 0:
  154.0 92.8 all-reduce.2
  499.2 247.1 all-reduce.4
where the time goes:
time: 756 us; the launch traced here: 755 us
  waiting for transfers between devices  615 us (81%)
  local copies, waits for them, and re-layouts  48.7 us (6%)
  other arithmetic  29.3 us (4%)
  starting transfers between devices  28.8 us (4%)
  matrix products  19.3 us (3%)
  between operations  14.2 us (2%)
    psum x1, waiting for transfers between devices, on_device(): lax.psum(local_weight, ('rows', 'rep')) * (1.0 / math.sqrt(node_total))  246 us
    all_to_all x1, waiting for transfers between devices, on_device(): lax.all_to_all(outgoing, 'rows', split_axis=0, concat_axis=0, tiled=True)  174 us
    all_to_all x1, waiting for transfers between devices, on_device(): lax.all_to_all(serve_blocks(mixed_rows, asked_places, block_size), 'rows'...  93.1 us
    psum x1, waiting for transfers between devices, on_device(): summed = lax.psum(partial_sum, 'rep')  92.9 us
    unnamed x14, local copies, waits for them, and re-layouts  19.2 us
  transfers between devices with their start and end apart: 5, of which 5 were waited for; matrix products, arithmetic and copies ran while one was open for 2% of the time, Pallas kernels for 0%

commit v1 on v0

--- a/solution.py
+++ b/solution.py
@@ -3,6 +3,7 @@
 import jax.numpy as jnp
 from jax import lax
 from jax.sharding import PartitionSpec as P
+from jax.lax import psum
 
 
 def silu_parts(summed):
@@ -98,7 +99,7 @@
     local_weight = jnp.dot(
         features.astype(jnp.float32).T, back_rows, precision=lax.Precision.HIGHEST
     )
-    weight_grad = lax.psum(local_weight, ("rows", "rep")) * (1.0 / math.sqrt(node_total))
+    weight_grad = psum(psum(local_weight, "rows"), "rep") * (1.0 / math.sqrt(node_total))
     input_grad = jnp.dot(
         back_rows.astype(jnp.bfloat16), weight.T, preferred_element_type=jnp.float32
     ).astype(jnp.bfloat16)

time: 756 us -> 727 us (0.962)
  waiting for transfers between devices: 615 us -> 585 us
    psum x1 -> x2, waiting for transfers between devices: 246 us -> 214 us  [the longest x1 168 us: on_device(): psum(local_weight, 'rows')]
  transfers between devices with their start and end apart: 5 -> 6, of which waited for: 5 -> 6; matrix products, arithmetic and copies ran while one was open for 2% -> 2% of each run, Pallas kernels for 0% -> 0%
where the time goes in v1:
time: 727 us; the launch traced here: 725 us
  waiting for transfers between devices  585 us (80%)
  local copies, waits for them, and re-layouts  48.9 us (7%)
  other arithmetic  29.3 us (4%)
  starting transfers between devices  28.8 us (4%)
  matrix products  19.3 us (3%)
  between operations  13.9 us (2%)
    all_to_all x1, waiting for transfers between devices, on_device(): lax.all_to_all(outgoing, 'rows', split_axis=0, concat_axis=0, tiled=True)  177 us
    psum x1, waiting for transfers between devices, on_device(): psum(local_weight, 'rows')  168 us
    all_to_all x1, waiting for transfers between devices, on_device(): lax.all_to_all(serve_blocks(mixed_rows, asked_places, block_size), 'rows'...  93.1 us
    psum x1, waiting for transfers between devices, on_device(): summed = lax.psum(partial_sum, 'rep')  92.9 us
    psum x1, waiting for transfers between devices, on_device(): psum(psum(local_weight, 'rows'), 'rep') * (1.0 / math.sqrt(node_total))  45.5 us
    unnamed x14, local copies, waits for them, and re-layouts  19.2 us
  transfers between devices with their start and end apart: 6, of which 6 were waited for; matrix products, arithmetic and copies ran while one was open for 2% of the time, Pallas kernels for 0%

profile of v1, /device:TPU:2, one launch (start us, length us, event | category | flops | bytes accessed | tf_op | source)
XLA Modules:
  0.0 725.1 jit_solution(11280827492853523220)
XLA Ops:
  9.3 12.1 %all-to-all-start = ((s32[64,1,1]{2,1,0:T(1,128)}), s32[64,1,1]{2,1,0:T(1,128)S(1)}, u32[]{:S(2)}, u32[]{:S(2)}) async-start(s32[64,1,1]{2,1,0:T(1,128)} %copy.38), calls=%async_computation | async-start | bytes 65536 | tf_op jit(solution)/shard_map/all_to_all | solution.py:55
  21.4 1.4 convolution_convert_fusion.1
  22.7 8.2 %all-to-all-done = s32[64,1,1]{2,1,0:T(1,128)S(1)} async-done(((s32[64,1,1]{2,1,0:T(1,128)}), s32[64,1,1]{2,1,0:T(1,128)S(1)}, u32[]{:S(2)}, u32[]{:S(2)}) %all-to-all-start) | async-done | bytes 288 | tf_op jit(solution)/shard_map/all_to_all | solution.py:55
  30.9 1.2 reduce.1
  32.1 2.8 gather_fusion.2
  34.9 1.2 compare_reduce_fusion
  36.1 4.0 select_select_fusion.2
  40.1 5.7 all-to-all-start.1
  46.1 2.8 gather_fusion.3
  48.9 93.1 %all-to-all-done.1 = bf16[64,128,256]{2,1,0:T(8,128)(2,1)} async-done(((bf16[64,128,256]{2,1,0:T(8,128)(2,1)}), bf16[64,128,256]{2,1,0:T(8,128)(2,1)}, u32[]{:S(2)}, u32[]{:S(2)}) %all-to-all-start.1) | async-done | bytes 4194336 | tf_op jit(solution)/shard_map/all_to_all | solution.py:57
  142.0 5.0 gather_fusion
  147.0 4.1 select_select_fusion.1
  151.0 2.8 fusion.2
  154.0 92.9 %all-reduce.4.cloned.1.call-done = f32[4096,256]{1,0:T(8,128)} async-done(((f32[4096,256]{1,0:T(8,128)}), f32[4096,256]{1,0:T(8,128)}) %all-reduce.4.cloned.1.call-update) | async-done | bytes 4194320 | tf_op jit(solution)/shard_map/psum | solution.py:71
  246.9 6.4 multiply_convert_fusion
  253.3 4.5 fusion
  257.9 9.0 %copy.41 = f32[64,128,256]{2,1,0:T(8,128)} copy(f32[64,128,256]{1,2,0:T(8,128)} %bitcast.59) | data formatting | bytes 16777216 | tf_op jit(solution)/shard_map/reshape | solution.py:80
  266.9 7.7 %gather_fusion.1 = f32[64,128,256]{2,1,0:T(8,128)} fusion(f32[64,128,256]{2,1,0:T(8,128)} %copy.41, s32[1024]{0:T(1024)S(1)} %pad_clamp_fusion), kind=kCustom, calls=%fused_computation.3 | custom fusion | bytes 16777472 | tf_op jit(solution)/shard_map/jit(_take)/gather | solution.py:84
  274.5 8.5 %select_select_fusion = f32[64,128,256]{2,1,0:T(8,128)} fusion(f32[64,128,256]{2,1,0:T(8,128)} %gather_fusion.1, pred[64]{0:T(512)(128)(4,1)S(1)} %compare_and_fusion.2, pred[64]{0:T(512)(128)(4,1)S(1)} %fusion.6), kind=kLoop, calls=%fused_computation.5 | loop fusion | flops 4194304 | bytes 16777344 | tf_op jit(solution)/shard_map/jit(_where)/select_n | solution.py:83
  283.0 10.7 %all-to-all-start.2 = ((f32[64,128,256]{2,1,0:T(8,128)}), f32[64,128,256]{2,1,0:T(8,128)}, u32[]{:S(2)}, u32[]{:S(2)}) async-start(f32[64,128,256]{2,1,0:T(8,128)} %select_select_fusion), calls=%async_computation.2 | async-start | bytes 16777216 | tf_op jit(solution)/shard_map/all_to_all | solution.py:86
  293.8 9.2 %copy.49 = f32[8,8,128,256]{3,1,2,0:T(8,128)} copy(f32[8,8,128,256]{2,3,1,0:T(8,128)} %bitcast.60) | data formatting | bytes 16777216
  303.0 176.8 %all-to-all-done.2 = f32[64,128,256]{2,1,0:T(8,128)} async-done(((f32[64,128,256]{2,1,0:T(8,128)}), f32[64,128,256]{2,1,0:T(8,128)}, u32[]{:S(2)}, u32[]{:S(2)}) %all-to-all-start.2) | async-done | bytes 8388640 | tf_op jit(solution)/shard_map/all_to_all | solution.py:86
  479.9 8.3 %copy.48 = f32[8,8,128,256]{3,1,2,0:T(8,128)S(1)} copy(f32[8,8,128,256]{3,2,1,0:T(8,128)} %bitcast.25) | data formatting | bytes 16777216
  488.1 2.9 fusion.8
  491.0 3.9 convolution_add_fusion
  494.9 1.5 reshape.298
  496.5 2.7 convolution_bitcast_fusion
  499.3 2.4 fusion.4
  501.7 168.4 %all-reduce.6.cloned.1.call-done = f32[256,256]{0,1:T(8,128)} async-done(((f32[256,256]{0,1:T(8,128)}), f32[256,256]{0,1:T(8,128)}) %all-reduce.6.cloned.1.call-update) | async-done | bytes 262160 | tf_op jit(solution)/shard_map/psum | solution.py:102
  670.1 1.1 convolution_convert_fusion
  671.3 45.5 %all-reduce.8.cloned.1.call-done = f32[256,256]{0,1:T(8,128)} async-done(((f32[256,256]{0,1:T(8,128)}), f32[256,256]{0,1:T(8,128)}) %all-reduce.8.cloned.1.call-update) | async-done | bytes 262160 | tf_op jit(solution)/shard_map/psum | solution.py:102
  716.8 1.0 broadcast_multiply_fusion
  (37 shorter events, 3.5 us)
Async XLA Ops:
  7.2 143.9 %copy-start = (bf16[32,1,2,128,128]{4,3,2,1,0:T(8,128)(2,1)S(1)}, bf16[32,1,2,128,128]{4,3,2,1,0:T(8,128)(2,1)}, u32[]{:S(2)}) copy-start(bf16[32,1,2,128,128]{4,3,2,1,0:T(8,128)(2,1)} %param.10) | copy-start | bytes 6291460
  9.3 21.6 %all-to-all-start = ((s32[64,1,1]{2,1,0:T(1,128)}), s32[64,1,1]{2,1,0:T(1,128)S(1)}, u32[]{:S(2)}, u32[]{:S(2)}) async-start(s32[64,1,1]{2,1,0:T(1,128)} %copy.38), calls=%async_computation | async-start | bytes 65536 | tf_op jit(solution)/shard_map/all_to_all | solution.py:55
  40.1 101.9 %all-to-all-start.1 = ((bf16[64,128,256]{2,1,0:T(8,128)(2,1)}), bf16[64,128,256]{2,1,0:T(8,128)(2,1)}, u32[]{:S(2)}, u32[]{:S(2)}) async-start(bf16[64,128,256]{2,1,0:T(8,128)(2,1)} %select_select_fusion.2), calls=%async_computation.1 | async-start | bytes 8388608 | tf_op jit(solution)/shard_map/all_to_all | solution.py:57
  45.8 201.1 %all-reduce.4.cloned.1.call-start = ((), (), s32[]{:S(2)}) async-start(), calls=%async_computation.3 | async-start | bytes 8388608 | tf_op jit(solution)/shard_map/psum | solution.py:71
  283.0 196.8 %all-to-all-start.2 = ((f32[64,128,256]{2,1,0:T(8,128)}), f32[64,128,256]{2,1,0:T(8,128)}, u32[]{:S(2)}, u32[]{:S(2)}) async-start(f32[64,128,256]{2,1,0:T(8,128)} %select_select_fusion), calls=%async_computation.2 | async-start | bytes 16777216 | tf_op jit(solution)/shard_map/all_to_all | solution.py:86
  293.8 376.3 %all-reduce.6.cloned.1.call-start = ((), (), s32[]{:S(2)}) async-start(), calls=%async_computation.4 | async-start | bytes 524288 | tf_op jit(solution)/shard_map/psum | solution.py:102
  479.8 11.2 %slice-start = ((s8[8388608]{0:T(1024)(128)(4,1)}), s8[4194304]{0:T(1024)(128)(4,1)S(1)}, s32[]{:S(2)}) async-start(s8[8388608]{0:T(1024)(128)(4,1)} %bitcast.63), calls=%async_computation.6 | async-start | bytes 8388608
  479.9 11.2 %slice-start.1 = ((s8[8388608]{0:T(1024)(128)(4,1)}), s8[4194304]{0:T(1024)(128)(4,1)S(1)}, s32[]{:S(2)}) async-start(s8[8388608]{0:T(1024)(128)(4,1)} %bitcast.63), calls=%async_computation.7 | async-start | bytes 8388608
  494.9 175.2 %copy-start.2 = (bf16[256,256]{1,0:T(8,128)(2,1)S(1)}, bf16[256,256]{1,0:T(8,128)(2,1)}, u32[]{:S(2)}) copy-start(bf16[256,256]{1,0:T(8,128)(2,1)} %param.8) | copy-start | bytes 393220
  494.9 223.7 %copy-start.1 = (bf16[32,1,2,128,128]{4,3,2,1,0:T(8,128)(2,1)S(1)}, bf16[32,1,2,128,128]{4,3,2,1,0:T(8,128)(2,1)}, u32[]{:S(2)}) copy-start(bf16[32,1,2,128,128]{4,3,2,1,0:T(8,128)(2,1)} %param.10) | copy-start | bytes 6291460
  499.2 217.6 %all-reduce.8.cloned.1.call-start = ((), (), s32[]{:S(2)}) async-start(), calls=%async_computation.5 | async-start | bytes 524288 | tf_op jit(solution)/shard_map/psum | solution.py:102
Sparse Core Ops, SparseCore 0:
  154.0 92.8 all-reduce.3
  499.4 170.6 all-reduce.5
  672.4 44.3 all-reduce.7
